TPU v7x, 256 devices: a whole 4x4x8 slice. The times are simulated.
256 devices in a mesh: section: 32 (over x, z), expert: 8 (over y, core).
Axes of the slice: x: 4, y: 4, z: 8, core: 2. Of those that a mesh axis runs over, the one named last changes fastest.
Arguments:
- tokens: bfloat16 [2048, 4096], P('expert', 'section'), may hold values from -6 to 6
- routes: int32 [2048, 2], P('expert'), may hold values from 0 to 7, all different within a row; in each aligned block of 256 rows (0 to 255, 256 to 511, ...) at most 80 rows name the same one
- mix_weights: float32 [2048, 2], P('expert'), may hold values from 0.2 to 1
- w_gate: bfloat16 [8, 4096, 8192], P('expert', None, 'section'), may hold values from -0.1875 to 0.1875
- w_up: bfloat16 [8, 4096, 8192], P('expert', None, 'section'), may hold values from -0.1875 to 0.1875
- w_down: bfloat16 [8, 8192, 4096], P('expert', 'section'), may hold values from -0.125 to 0.125
- upstream: bfloat16 [2048, 4096], P('expert', 'section'), may hold values from -6 to 6
Outputs:
- mixed: bfloat16 [2048, 4096], P('expert', 'section')
- grad_tokens: bfloat16 [2048, 4096], P('expert', 'section')
- grad_mix: float32 [2048, 2], P('expert')
- grad_gate: bfloat16 [8, 4096, 8192], P('expert', None, 'section')
- grad_up: bfloat16 [8, 4096, 8192], P('expert', None, 'section')
- grad_down: bfloat16 [8, 8192, 4096], P('expert', 'section')
Inputs may be any that keep to these rules, and one draw needn't show every extreme that they name: `routes`: each token names 2 different experts. Among the 256 tokens of one index of the expert axis no expert is named more than 80 times, and in some such block one expert is named exactly 80 times.
All inputs are finite; a program needn't handle non-finite values.
Results may differ from a plain program's by a relative error of at most 0.02.
Values may be sent and summed in bfloat16 or wider, within the bound.
No kernel may reach another device: no remote copies, remote signals or barrier semaphores. Data moves between devices by JAX's collectives and lax.ppermute only.
A program may use at most 128 MiB of HBM per device.

v0:
```python
import jax
import jax.numpy as jnp
from jax import lax
from jax.sharding import PartitionSpec as P

highest = lax.Precision.HIGHEST


def slot_tables(route_rows, mix_rows, capacity, experts):
    tok_count, top_count = route_rows.shape
    flat_routes = route_rows.reshape(-1)
    onehot = (flat_routes[:, None] == jnp.arange(experts, dtype=jnp.int32)[None, :]).astype(
        jnp.int32
    )
    earlier = jnp.cumsum(onehot, axis=0) - onehot
    position = jnp.sum(earlier * onehot, axis=1)
    target = (flat_routes * capacity + position).reshape(tok_count, top_count)
    slot_ids = jnp.arange(experts * capacity, dtype=jnp.int32)
    hits = target[None, :, :] == slot_ids[:, None, None]
    matches = hits.astype(jnp.float32)
    select = jnp.sum(matches, axis=2)
    weighted = jnp.sum(matches * mix_rows[None, :, :], axis=2)
    token_ids = jnp.arange(tok_count, dtype=jnp.int32)
    slot_token = jnp.sum(jnp.sum(hits.astype(jnp.int32), axis=2) * token_ids[None, :], axis=1)
    return (target, select, weighted, slot_token)


def per_device(tokens, routes, mix_weights, w_gate, w_up, w_down, upstream):
    experts = lax.axis_size("expert")
    tok_count = tokens.shape[0]
    top_count = routes.shape[1]
    capacity = 5 * tok_count * top_count // (4 * experts)
    slot_total = experts * capacity
    target, select, weighted, slot_token = slot_tables(routes, mix_weights, capacity, experts)
    slot_fill = jnp.sum(select, axis=1)
    slot_scale = jnp.sum(weighted, axis=1)
    gate_local = w_gate[0]
    up_local = w_up[0]
    down_local = w_down[0]

    def collect(source, factor):
        taken = source[slot_token].astype(jnp.float32)
        return (taken * factor[:, None]).astype(jnp.bfloat16)

    def to_experts(source, factor):
        block = collect(source, factor)
        arrived = lax.all_to_all(
            block.reshape(experts, capacity, -1), "expert", split_axis=0, concat_axis=0, tiled=True
        )
        whole = lax.all_gather(arrived, "section", axis=2, tiled=True)
        return whole.reshape(slot_total, -1)

    def to_sources(partial_value):
        summed = lax.psum_scatter(
            partial_value.reshape(experts, capacity, -1).astype(jnp.bfloat16),
            "section",
            scatter_dimension=2,
            tiled=True,
        )
        back = lax.all_to_all(summed, "expert", split_axis=0, concat_axis=0, tiled=True)
        return back.reshape(slot_total, -1)

    dispatched = to_experts(tokens, slot_fill)
    act_gate = jnp.dot(dispatched, gate_local, preferred_element_type=jnp.float32)
    act_up = jnp.dot(dispatched, up_local, preferred_element_type=jnp.float32)
    sig = jax.nn.sigmoid(act_gate)
    silu_gate = act_gate * sig
    hidden = (silu_gate * act_up).astype(jnp.bfloat16)
    partial_value = jnp.dot(hidden, down_local, preferred_element_type=jnp.float32)
    returned = to_sources(partial_value).astype(jnp.float32)
    moe_out = jnp.dot(weighted.T, returned, precision=highest)
    mixed = (tokens.astype(jnp.float32) + moe_out).astype(jnp.bfloat16)
    picked = returned[target]
    upstream_wide = upstream.astype(jnp.float32)
    mix_terms = jnp.einsum("tkd,td->tk", picked, upstream_wide, precision=highest)
    grad_mix = lax.psum(mix_terms, "section")
    grad_rows = to_experts(upstream, slot_scale)
    grad_hidden = lax.dot_general(
        grad_rows, down_local, (((1,), (1,)), ((), ())), preferred_element_type=jnp.float32
    )
    grad_down = lax.dot_general(
        hidden, grad_rows, (((0,), (0,)), ((), ())), preferred_element_type=jnp.float32
    ).astype(jnp.bfloat16)
    dsilu = sig * (1.0 + act_gate * (1.0 - sig))
    grad_act_gate = (grad_hidden * act_up * dsilu).astype(jnp.bfloat16)
    grad_act_up = (grad_hidden * silu_gate).astype(jnp.bfloat16)
    grad_gate = lax.dot_general(
        dispatched, grad_act_gate, (((0,), (0,)), ((), ())), preferred_element_type=jnp.float32
    ).astype(jnp.bfloat16)
    grad_up = lax.dot_general(
        dispatched, grad_act_up, (((0,), (0,)), ((), ())), preferred_element_type=jnp.float32
    ).astype(jnp.bfloat16)
    first = lax.dot_general(
        grad_act_gate, gate_local, (((1,), (1,)), ((), ())), preferred_element_type=jnp.float32
    )
    second = lax.dot_general(
        grad_act_up, up_local, (((1,), (1,)), ((), ())), preferred_element_type=jnp.float32
    )
    back_rows = to_sources(first + second).astype(jnp.float32)
    grad_moe = jnp.dot(select.T, back_rows, precision=highest)
    grad_tokens = (upstream_wide + grad_moe).astype(jnp.bfloat16)
    return (mixed, grad_tokens, grad_mix, grad_gate[None], grad_up[None], grad_down[None])


def solution(mesh):
    return jax.shard_map(
        per_device,
        mesh=mesh,
        in_specs=(
            P("expert", "section"),
            P("expert", None),
            P("expert", None),
            P("expert", None, "section"),
            P("expert", None, "section"),
            P("expert", "section", None),
            P("expert", "section"),
        ),
        out_specs=(
            P("expert", "section"),
            P("expert", "section"),
            P("expert", None),
            P("expert", None, "section"),
            P("expert", None, "section"),
            P("expert", "section", None),
        ),
        check_vma=False,
    )
```

profile of v0, /device:TPU:8, one launch (start us, length us, event | category | flops | bytes accessed | tf_op | source)
XLA Modules:
  0.0 783.5 jit_solution(15971595313948356913)
XLA Ops:
  11.4 2.1 select_reduce_fusion
  15.7 10.3 %all_to_all.20 = bf16[8,80,128]{2,1,0:T(8,128)(2,1)} all-to-all(bf16[8,80,128]{2,1,0:T(8,128)(2,1)S(1)} %fusion.17), channel_id=1, replica_groups=mesh['section'=32,'expert'=8] {'expert'}, dimensions={0} | all-to-all | bytes 327680 | tf_op jit(solution)/shard_map/all_to_all | solution.py:47
  28.3 9.5 %all_to_all.21 = bf16[8,80,128]{2,1,0:T(8,128)(2,1)} all-to-all(bf16[8,80,128]{2,1,0:T(8,128)(2,1)S(1)} %fusion.16), channel_id=1, replica_groups=mesh['section'=32,'expert'=8] {'expert'}, dimensions={0} | all-to-all | bytes 327680 | tf_op jit(solution)/shard_map/all_to_all | solution.py:47
  37.9 77.2 %all-gather.3.cloned.1.call-done = bf16[8,80,4096]{2,1,0:T(8,128)(2,1)} async-done(((bf16[8,80,128]{2,1,0:T(8,128)(2,1)}), bf16[8,80,4096]{2,1,0:T(8,128)(2,1)}) %all-gather.3.cloned.1.call-update) | async-done | bytes 5242896 | tf_op jit(solution)/shard_map/all_gather | solution.py:50
  115.2 5.7 fusion.7
  120.8 2.4 fusion.11
  123.2 81.6 %all-gather.5.cloned.1.call-done = bf16[8,80,4096]{2,1,0:T(8,128)(2,1)} async-done(((bf16[8,80,128]{2,1,0:T(8,128)(2,1)}), bf16[8,80,4096]{2,1,0:T(8,128)(2,1)}) %all-gather.5.cloned.1.call-update) | async-done | bytes 5242896 | tf_op jit(solution)/shard_map/all_gather | solution.py:50
  204.7 5.4 multiply_convert_fusion
  210.1 3.9 convolution_convert_fusion
  214.0 11.2 %copy.36 = bf16[8,80,4096]{1,0,2:T(8,128)(2,1)} copy(bf16[8,80,4096]{2,1,0:T(8,128)(2,1)} %convolution_convert_fusion) | data formatting | bytes 10485760
  225.2 13.1 %reshape.124 = bf16[4096,640]{1,0:T(8,128)(2,1)} reshape(bf16[4096,8,80]{2,1,0:T(8,128)(2,1)} %bitcast.66) | data formatting | bytes 10485760
  239.8 2.7 fusion.9
  242.5 3.9 add_convert_fusion
  246.4 11.2 %copy.38 = bf16[8,80,4096]{1,0,2:T(8,128)(2,1)} copy(bf16[8,80,4096]{2,1,0:T(8,128)(2,1)} %bitcast.69) | data formatting | bytes 10485760
  257.6 13.1 %reshape.126 = bf16[4096,640]{1,0:T(8,128)(2,1)} reshape(bf16[4096,8,80]{2,1,0:T(8,128)(2,1)} %bitcast.67) | data formatting | bytes 10485760
  271.7 5.7 fusion.1
  277.4 5.8 fusion
  283.2 180.6 %reduce-scatter.7.cloned.1.call-done = bf16[128,640]{1,0:T(8,128)(2,1)} async-done(((bf16[4096,640]{1,0:T(8,128)(2,1)}), bf16[128,640]{1,0:T(8,128)(2,1)}) %reduce-scatter.7.cloned.1.call-update) | async-done | bytes 163856
  465.8 4.8 all-to-all-start.1
  470.6 5.8 fusion.2
  476.4 215.3 %reduce-scatter.9.cloned.1.call-done = bf16[128,640]{1,0:T(8,128)(2,1)} async-done(((bf16[4096,640]{1,0:T(8,128)(2,1)}), bf16[128,640]{1,0:T(8,128)(2,1)}) %reduce-scatter.9.cloned.1.call-update) | async-done | bytes 163856
  693.7 4.8 all-to-all-start.3
  700.3 72.8 %psum.7 = f32[256,2]{0,1:T(2,128)} all-reduce(f32[256,2]{0,1:T(2,128)S(1)} %bitcast.81), channel_id=1, replica_groups=mesh['section'=32,'expert'=8] {'section'}, use_global_device_ids=true, to_apply=%region_11.12 | all-reduce | flops 512 | bytes 4096 | tf_op jit(solution)/shard_map/psum | solution.py:76
  773.2 2.4 fusion.13
  (65 shorter events, 18.5 us)
Async XLA Ops:
  7.2 197.6 %copy-start = (bf16[1,256,4096]{2,1,0:T(8,128)(2,1)S(1)}, bf16[1,256,4096]{2,1,0:T(8,128)(2,1)}, u32[]{:S(2)}) copy-start(bf16[1,256,4096]{2,1,0:T(8,128)(2,1)} %param.12) | copy-start | bytes 6291460
  7.2 6.4 copy-start.2
  7.2 18.9 %copy-start.3 = (bf16[256,128]{1,0:T(8,128)(2,1)S(1)}, bf16[256,128]{1,0:T(8,128)(2,1)}, u32[]{:S(2)}) copy-start(bf16[256,128]{1,0:T(8,128)(2,1)} %param.13) | copy-start | bytes 196612
  7.2 108.0 %all-gather.3.cloned.1.call-start = ((), (), s32[]{:S(2)}) async-start(), calls=%async_computation.6 | async-start | bytes 5406720 | tf_op jit(solution)/shard_map/all_gather | solution.py:50
  26.0 178.7 %all-gather.5.cloned.1.call-start = ((), (), s32[]{:S(2)}) async-start(), calls=%async_computation.7 | async-start | bytes 5406720 | tf_op jit(solution)/shard_map/all_gather | solution.py:50
  37.9 425.9 %reduce-scatter.7.cloned.1.call-start = ((), (), s32[]{:S(2)}) async-start(), calls=%async_computation.8 | async-start | bytes 5406720
  115.2 5.7 copy-start.4
  115.2 5.7 copy-start.10
  238.2 1.6 copy-start.5
  238.3 453.4 %reduce-scatter.9.cloned.1.call-start = ((), (), s32[]{:S(2)}) async-start(), calls=%async_computation.9 | async-start | bytes 5406720
  239.8 2.7 copy-start.6
  239.8 2.7 copy-start.8
  270.7 1.0 copy-start.9
  271.7 5.7 copy-start.7
  465.8 227.9 %all-to-all-start.1 = ((bf16[8,80,128]{2,1,0:T(8,128)(2,1)}), bf16[8,80,128]{2,1,0:T(8,128)(2,1)S(1)}, u32[]{:S(2)}, u32[]{:S(2)}) async-start(bf16[8,80,128]{2,1,0:T(8,128)(2,1)} %copy.37), calls=%async_computation.1 | async-start | bytes 327680 | tf_op jit(solution)/shard_map/all_to_all | solution.py:60
  470.6 306.3 %copy-start.1 = (bf16[1,256,4096]{2,1,0:T(8,128)(2,1)S(1)}, bf16[1,256,4096]{2,1,0:T(8,128)(2,1)}, u32[]{:S(2)}) copy-start(bf16[1,256,4096]{2,1,0:T(8,128)(2,1)} %param.12) | copy-start | bytes 6291460
  693.7 81.9 %all-to-all-start.3 = ((bf16[8,80,128]{2,1,0:T(8,128)(2,1)}), bf16[8,80,128]{2,1,0:T(8,128)(2,1)S(1)}, u32[]{:S(2)}, u32[]{:S(2)}) async-start(bf16[8,80,128]{2,1,0:T(8,128)(2,1)} %copy.39), calls=%async_computation.3 | async-start | bytes 327680 | tf_op jit(solution)/shard_map/all_to_all | solution.py:60
Sparse Core Ops, SparseCore 0:
  26.1 88.9 all-gather.2
  117.6 87.0 all-gather.4
  238.4 225.3 reduce-scatter.6
  467.6 224.0 reduce-scatter.8
where the time goes:
time: 785 us; the launch traced here: 783 us
  waiting for transfers between devices  555 us (71%)
  blocking collectives  92.6 us (12%)
  local copies, waits for them, and re-layouts  62.1 us (8%)
  matrix products  45.3 us (6%)
  between operations  14 us (2%)
  starting transfers between devices  9.93 us (1%)
    unnamed x6, waiting for transfers between devices  396 us
    all_gather x2, waiting for transfers between devices, to_experts(): whole = lax.all_gather(arrived, 'section', axis=2, tiled=True)  159 us
    psum x1, blocking collectives, per_device(): grad_mix = lax.psum(mix_terms, 'section')  72.8 us
    unnamed x31, local copies, waits for them, and re-layouts  55.6 us
    all_to_all x2, blocking collectives, to_experts(): lax.all_to_all(block.reshape(experts, capacity, -1), 'expert', split_axis...  19.8 us
  transfers between devices with their start and end apart: 6, of which 4 were waited for; matrix products, arithmetic and copies ran while one was open for 9% of the time, Pallas kernels for 0%

commit v1 on v0

--- a/solution.py
+++ b/solution.py
@@ -73,7 +73,11 @@
     picked = returned[target]
     upstream_wide = upstream.astype(jnp.float32)
     mix_terms = jnp.einsum("tkd,td->tk", picked, upstream_wide, precision=highest)
-    grad_mix = lax.psum(mix_terms, "section")
+    grad_mix = mix_terms
+    for hop in (1, 2, 4, 8, 16):
+        grad_mix = grad_mix + lax.ppermute(
+            grad_mix, "section", [(dev, dev ^ hop) for dev in range(32)]
+        )
     grad_rows = to_experts(upstream, slot_scale)
     grad_hidden = lax.dot_general(
         grad_rows, down_local, (((1,), (1,)), ((), ())), preferred_element_type=jnp.float32

time: 785 us -> 716 us (0.912)
  blocking collectives: 92.6 us -> 19.8 us
  starting transfers between devices: 9.93 us -> 18.8 us
    psum x1 -> x0, blocking collectives: 72.8 us -> none  [per_device(): grad_mix = lax.psum(mix_terms, 'section')]
    ppermute x0 -> x5, starting transfers between devices: none -> 8.81 us  [per_device(): lax.ppermute(grad_mix, 'section', [(dev, dev ^ hop) for dev in range(32)])]
    unnamed x31 -> x39, local copies, waits for them, and re-layouts: 55.6 us -> 55 us
  transfers between devices with their start and end apart: 6 -> 11, of which waited for: 4 -> 7; matrix products, arithmetic and copies ran while one was open for 9% -> 9% of each run, Pallas kernels for 0% -> 0%
where the time goes in v1:
time: 716 us; the launch traced here: 714 us
  waiting for transfers between devices  554 us (77%)
  local copies, waits for them, and re-layouts  61.5 us (9%)
  matrix products  40.4 us (6%)
  blocking collectives  19.8 us (3%)
  starting transfers between devices  18.8 us (3%)
  between operations  14 us (2%)
    unnamed x6, waiting for transfers between devices  389 us
    all_gather x2, waiting for transfers between devices, to_experts(): whole = lax.all_gather(arrived, 'section', axis=2, tiled=True)  159 us
    unnamed x39, local copies, waits for them, and re-layouts  55 us
    all_to_all x2, blocking collectives, to_experts(): lax.all_to_all(block.reshape(experts, capacity, -1), 'expert', split_axis...  19.8 us
  transfers between devices with their start and end apart: 11, of which 7 were waited for; matrix products, arithmetic and copies ran while one was open for 9% of the time, Pallas kernels for 0%

profile of v1, /device:TPU:8, one launch (start us, length us, event | category | flops | bytes accessed | tf_op | source)
XLA Modules:
  0.0 714.2 jit_solution(3954726751920810985)
XLA Ops:
  15.7 10.3 %all_to_all.20 = bf16[8,80,128]{2,1,0:T(8,128)(2,1)} all-to-all(bf16[8,80,128]{2,1,0:T(8,128)(2,1)S(1)} %fusion.17), channel_id=1, replica_groups=mesh['section'=32,'expert'=8] {'expert'}, dimensions={0} | all-to-all | bytes 327680 | tf_op jit(solution)/shard_map/all_to_all | solution.py:47
  28.3 9.6 %all_to_all.21 = bf16[8,80,128]{2,1,0:T(8,128)(2,1)} all-to-all(bf16[8,80,128]{2,1,0:T(8,128)(2,1)S(1)} %fusion.16), channel_id=1, replica_groups=mesh['section'=32,'expert'=8] {'expert'}, dimensions={0} | all-to-all | bytes 327680 | tf_op jit(solution)/shard_map/all_to_all | solution.py:47
  37.9 77.2 %all-gather.3.cloned.1.call-done = bf16[8,80,4096]{2,1,0:T(8,128)(2,1)} async-done(((bf16[8,80,128]{2,1,0:T(8,128)(2,1)}), bf16[8,80,4096]{2,1,0:T(8,128)(2,1)}) %all-gather.3.cloned.1.call-update) | async-done | bytes 5242896 | tf_op jit(solution)/shard_map/all_gather | solution.py:50
  115.1 5.7 fusion.7
  123.2 81.6 %all-gather.5.cloned.1.call-done = bf16[8,80,4096]{2,1,0:T(8,128)(2,1)} async-done(((bf16[8,80,128]{2,1,0:T(8,128)(2,1)}), bf16[8,80,4096]{2,1,0:T(8,128)(2,1)}) %all-gather.5.cloned.1.call-update) | async-done | bytes 5242896 | tf_op jit(solution)/shard_map/all_gather | solution.py:50
  204.7 5.4 multiply_convert_fusion
  210.1 3.8 convolution_convert_fusion
  213.9 11.2 %copy.36 = bf16[8,80,4096]{1,0,2:T(8,128)(2,1)} copy(bf16[8,80,4096]{2,1,0:T(8,128)(2,1)} %convolution_convert_fusion) | data formatting | bytes 10485760
  225.1 13.1 %reshape.124 = bf16[4096,640]{1,0:T(8,128)(2,1)} reshape(bf16[4096,8,80]{2,1,0:T(8,128)(2,1)} %bitcast.67) | data formatting | bytes 10485760
  239.8 2.7 fusion.9
  242.5 3.8 add_convert_fusion
  246.4 11.2 %copy.38 = bf16[8,80,4096]{1,0,2:T(8,128)(2,1)} copy(bf16[8,80,4096]{2,1,0:T(8,128)(2,1)} %bitcast.70) | data formatting | bytes 10485760
  257.5 13.1 %reshape.126 = bf16[4096,640]{1,0:T(8,128)(2,1)} reshape(bf16[4096,8,80]{2,1,0:T(8,128)(2,1)} %bitcast.68) | data formatting | bytes 10485760
  270.7 193.2 %reduce-scatter.7.cloned.1.call-done = bf16[128,640]{1,0:T(8,128)(2,1)} async-done(((bf16[4096,640]{1,0:T(8,128)(2,1)}), bf16[128,640]{1,0:T(8,128)(2,1)}) %reduce-scatter.7.cloned.1.call-update) | async-done | bytes 163856
  465.9 4.8 all-to-all-start.1
  471.1 4.7 all-to-all-done.1
  478.3 6.0 fusion.1
  484.4 2.4 collective-permute-start.1
  486.7 3.2 fusion
  490.0 3.0 collective-permute-start.2
  493.0 3.2 fusion.2
  496.2 195.3 %reduce-scatter.9.cloned.1.call-done = bf16[128,640]{1,0:T(8,128)(2,1)} async-done(((bf16[4096,640]{1,0:T(8,128)(2,1)}), bf16[128,640]{1,0:T(8,128)(2,1)}) %reduce-scatter.9.cloned.1.call-update) | async-done | bytes 163856
  693.5 4.8 all-to-all-start.3
  699.0 2.4 fusion.13
  (89 shorter events, 28.5 us)
Async XLA Ops:
  7.2 197.6 %copy-start = (bf16[1,256,4096]{2,1,0:T(8,128)(2,1)S(1)}, bf16[1,256,4096]{2,1,0:T(8,128)(2,1)}, u32[]{:S(2)}) copy-start(bf16[1,256,4096]{2,1,0:T(8,128)(2,1)} %param.12) | copy-start | bytes 6291460
  7.2 6.4 copy-start.2
  7.2 18.9 %copy-start.3 = (bf16[256,128]{1,0:T(8,128)(2,1)S(1)}, bf16[256,128]{1,0:T(8,128)(2,1)}, u32[]{:S(2)}) copy-start(bf16[256,128]{1,0:T(8,128)(2,1)} %param.13) | copy-start | bytes 196612
  7.2 107.9 %all-gather.3.cloned.1.call-start = ((), (), s32[]{:S(2)}) async-start(), calls=%async_computation.6 | async-start | bytes 5406720 | tf_op jit(solution)/shard_map/all_gather | solution.py:50
  26.0 178.7 %all-gather.5.cloned.1.call-start = ((), (), s32[]{:S(2)}) async-start(), calls=%async_computation.7 | async-start | bytes 5406720 | tf_op jit(solution)/shard_map/all_gather | solution.py:50
  37.9 426.0 %reduce-scatter.7.cloned.1.call-start = ((), (), s32[]{:S(2)}) async-start(), calls=%async_computation.8 | async-start | bytes 5406720
  115.1 5.7 copy-start.4
  115.1 5.7 copy-start.10
  238.2 453.2 %reduce-scatter.9.cloned.1.call-start = ((), (), s32[]{:S(2)}) async-start(), calls=%async_computation.9 | async-start | bytes 5406720
  239.8 2.7 copy-start.8
  270.6 207.7 %copy-start.9 = (bf16[640,256]{1,0:T(8,128)(2,1)S(1)}, bf16[640,256]{1,0:T(8,128)(2,1)}, u32[]{:S(2)}) copy-start(bf16[640,256]{1,0:T(8,128)(2,1)} %get-tuple-element.12) | copy-start | bytes 983044
  465.9 9.8 %all-to-all-start.1 = ((bf16[8,80,128]{2,1,0:T(8,128)(2,1)}), bf16[8,80,128]{2,1,0:T(8,128)(2,1)S(1)}, u32[]{:S(2)}, u32[]{:S(2)}) async-start(bf16[8,80,128]{2,1,0:T(8,128)(2,1)} %copy.37), calls=%async_computation.1 | async-start | bytes 327680 | tf_op jit(solution)/shard_map/all_to_all | solution.py:60
  477.6 9.1 %slice-start.2 = ((s8[5242880]{0:T(1024)(128)(4,1)}), s8[4194304]{0:T(1024)(128)(4,1)S(1)}, s32[]{:S(2)}) async-start(s8[5242880]{0:T(1024)(128)(4,1)} %bitcast.88), calls=%async_computation.12 | async-start | bytes 8388608
  477.6 9.1 %copy-start.7 = (bf16[640,256]{1,0:T(8,128)(2,1)S(1)}, bf16[640,256]{1,0:T(8,128)(2,1)}, u32[]{:S(2)}) copy-start(bf16[640,256]{1,0:T(8,128)(2,1)} %get-tuple-element.13) | copy-start | bytes 983044
  477.6 9.1 %slice-start.3 = ((s8[5242880]{0:T(1024)(128)(4,1)}), s8[1048576]{0:T(1024)(128)(4,1)S(1)}, s32[]{:S(2)}) async-start(s8[5242880]{0:T(1024)(128)(4,1)} %bitcast.88), calls=%async_computation.13 | async-start | bytes 2097152
  477.6 6.7 collective-permute-start
  484.3 8.6 %slice-start = ((s8[5242880]{0:T(1024)(128)(4,1)}), s8[4194304]{0:T(1024)(128)(4,1)S(1)}, s32[]{:S(2)}) async-start(s8[5242880]{0:T(1024)(128)(4,1)} %bitcast.72), calls=%async_computation.10 | async-start | bytes 8388608
  484.3 8.6 %slice-start.1 = ((s8[5242880]{0:T(1024)(128)(4,1)}), s8[1048576]{0:T(1024)(128)(4,1)S(1)}, s32[]{:S(2)}) async-start(s8[5242880]{0:T(1024)(128)(4,1)} %bitcast.72), calls=%async_computation.11 | async-start | bytes 2097152
  484.4 5.6 collective-permute-start.1
  490.0 208.3 %collective-permute-start.2 = (f32[256,2]{0,1:T(2,128)S(1)}, f32[256,2]{0,1:T(2,128)S(1)}, u32[]{:S(2)}, u32[]{:S(2)}) collective-permute-start(f32[256,2]{0,1:T(2,128)S(1)} %add.67), channel_id=1, source_target_pairs={{0,32},{8,40},{16,48},{24,56},{32,0},{40,8},{48,16},{56,24},{64,96... | collective-permute-start | bytes 6152 | tf_op jit(solution)/shard_map/ppermute | solution.py:78
  493.0 214.7 %copy-start.1 = (bf16[1,256,4096]{2,1,0:T(8,128)(2,1)S(1)}, bf16[1,256,4096]{2,1,0:T(8,128)(2,1)}, u32[]{:S(2)}) copy-start(bf16[1,256,4096]{2,1,0:T(8,128)(2,1)} %param.12) | copy-start | bytes 6291460
  693.5 10.6 %all-to-all-start.3 = ((bf16[8,80,128]{2,1,0:T(8,128)(2,1)}), bf16[8,80,128]{2,1,0:T(8,128)(2,1)S(1)}, u32[]{:S(2)}, u32[]{:S(2)}) async-start(bf16[8,80,128]{2,1,0:T(8,128)(2,1)} %copy.39), calls=%async_computation.3 | async-start | bytes 327680 | tf_op jit(solution)/shard_map/all_to_all | solution.py:60
  698.3 3.7 collective-permute-start.3
  702.0 5.1 collective-permute-start.4
  (2 other events, 4.3 us)
Sparse Core Ops, SparseCore 0:
  26.1 88.9 all-gather.2
  117.6 87.0 all-gather.4
  238.4 225.4 reduce-scatter.6
  467.7 223.7 reduce-scatter.8
